TPU v7x, 256 devices: a whole 4x4x8 slice. The times are simulated.
256 devices in a mesh: seq: 32 (over y, z_hi, core), col: 8 (over x, z_lo).
Axes of the slice: x: 4, y: 4, z: 8 (z_hi: 4, z_lo: 2; z = z_hi * 2 + z_lo), core: 2. Of those that a mesh axis runs over, the one named last changes fastest.
Arguments:
- memory: bfloat16 [4096, 4096], P('col', 'seq'), may hold values from -8 to 8
- query: bfloat16 [8192, 2048], P('seq', 'col'), may hold values from -400 to 400
- out_grad: bfloat16 [8192, 2048], P('seq', 'col'), may hold values from -96 to 96
- w_key: bfloat16 [4096, 2048], P(None, 'col'), may hold values from -0.09375 to 0.09375
- w_value: bfloat16 [4096, 2048], P(None, 'col'), may hold values from -0.09375 to 0.09375
Outputs:
- d_query: bfloat16 [8192, 2048], P('seq', 'col')
- d_memory: bfloat16 [4096, 4096], P('col', 'seq')
All inputs are finite; a program needn't handle non-finite values.
Results may differ from a plain program's by a relative error of at most 0.02.
The roundings to bfloat16 on the way count: a program that leaves them out, or rounds other values in their place, can miss the bound.
Values may be sent and summed in bfloat16 or wider, within the bound.
A program may use at most 128 MiB of HBM per device.

v0:
```python
import math

import jax
import jax.numpy as jnp
from jax import lax
from jax.sharding import PartitionSpec as P

HD = 64


def joined_along(pieces, dim):
    lengths = list(pieces.shape[1:])
    lengths[dim] *= pieces.shape[0]
    return jnp.moveaxis(pieces, 0, dim).reshape(lengths)


def sent_to_all(array, axis):
    devices = lax.axis_size(axis)
    return lax.all_to_all(
        jnp.broadcast_to(array[None], (devices, *array.shape)), axis, 0, 0, tiled=True
    )


def collect(array, axis, dim):
    return joined_along(sent_to_all(array, axis), dim)


def in_one_piece(arrays, axis, dim, along):
    ends, at = ([], 0)
    for a in arrays[:-1]:
        at += a.shape[along]
        ends.append(at)
    both = jnp.concatenate(arrays, axis=along)
    return tuple(jnp.split(lax.all_gather(both, axis, axis=dim, tiled=True), ends, axis=along))


def side_by_side(arrays, axis, dim, along):
    both = jnp.concatenate(arrays, axis=along)
    whole, at, outs = (lax.psum_scatter(both, axis, scatter_dimension=dim, tiled=True), 0, [])
    for a in arrays:
        outs.append(lax.slice_in_dim(whole, at, at + a.shape[along], axis=along))
        at += a.shape[along]
    return tuple(outs)


def split_up(array, dim, devices):
    before, after = (array.shape[:dim], array.shape[dim + 1 :])
    return jnp.moveaxis(array.reshape(*before, devices, -1, *after), dim, 0)


def sum_at_owner(array, axis, dim):
    devices = lax.axis_size(axis)
    pieces = lax.all_to_all(split_up(array, dim, devices), axis, 0, 0, tiled=True)
    return jnp.sum(pieces.astype(jnp.float32), axis=0)


def local(memory, query, out_grad, w_key, w_value):
    factor = 1.0 / math.sqrt(HD)
    dealt = lax.all_to_all(memory, "seq", split_axis=0, concat_axis=1, tiled=True)
    mem_local = collect(dealt, "col", 0)
    key_local = jnp.dot(mem_local, w_key, preferred_element_type=jnp.float32).astype(jnp.bfloat16)
    value_local = jnp.dot(mem_local, w_value, preferred_element_type=jnp.float32).astype(
        jnp.bfloat16
    )
    tgt_rows = query.shape[0]
    local_width = query.shape[1]
    heads_local = local_width // HD
    key_all, value_all = in_one_piece((key_local, value_local), "seq", 0, 1)
    total_src = key_all.shape[0]
    query_heads = query.reshape(tgt_rows, heads_local, HD)
    grad_heads = out_grad.reshape(tgt_rows, heads_local, HD)
    key_heads = key_all.reshape(total_src, heads_local, HD)
    value_heads = value_all.reshape(total_src, heads_local, HD)
    scores = (
        jnp.einsum("qhd,khd->hqk", query_heads, key_heads, preferred_element_type=jnp.float32)
        * factor
    )
    row_max = jnp.max(scores, axis=-1, keepdims=True)
    expo = jnp.exp(scores - row_max)
    weights = expo / jnp.sum(expo, axis=-1, keepdims=True)
    weights_low = weights.astype(jnp.bfloat16)
    attended = jnp.einsum(
        "hqk,khd->qhd", weights_low, value_heads, preferred_element_type=jnp.float32
    )
    row_delta = jnp.sum(grad_heads.astype(jnp.float32) * attended, axis=-1).T
    prob_grad = jnp.einsum(
        "qhd,khd->hqk", grad_heads, value_heads, preferred_element_type=jnp.float32
    )
    score_grad = (weights * (prob_grad - row_delta[..., None]) * factor).astype(jnp.bfloat16)
    query_grad = jnp.einsum(
        "hqk,khd->qhd", score_grad, key_heads, preferred_element_type=jnp.float32
    )
    d_query = query_grad.reshape(tgt_rows, local_width).astype(jnp.bfloat16)
    key_part = jnp.einsum(
        "hqk,qhd->khd", score_grad, query_heads, preferred_element_type=jnp.float32
    ).reshape(total_src, local_width)
    value_part = jnp.einsum(
        "hqk,qhd->khd", weights_low, grad_heads, preferred_element_type=jnp.float32
    ).reshape(total_src, local_width)
    key_sum, value_sum = tuple(
        (
            part.astype(jnp.float32)
            for part in side_by_side(
                (key_part.astype(jnp.bfloat16), value_part.astype(jnp.bfloat16)), "seq", 0, 1
            )
        )
    )
    key_low = key_sum.astype(jnp.bfloat16)
    value_low = value_sum.astype(jnp.bfloat16)
    partial_value = jnp.einsum("ri,di->rd", key_low, w_key, preferred_element_type=jnp.float32)
    partial_value = partial_value + jnp.einsum(
        "ri,di->rd", value_low, w_value, preferred_element_type=jnp.float32
    )
    summed = sum_at_owner(partial_value.astype(jnp.bfloat16), "col", 0).astype(jnp.bfloat16)
    d_memory = lax.all_to_all(summed, "seq", split_axis=1, concat_axis=0, tiled=True)
    return (d_query, d_memory)


def solution(mesh):
    return jax.shard_map(
        local,
        mesh=mesh,
        in_specs=(
            P("col", "seq"),
            P("seq", "col"),
            P("seq", "col"),
            P(None, "col"),
            P(None, "col"),
        ),
        out_specs=(P("seq", "col"), P("col", "seq")),
        check_vma=False,
    )
```

profile of v0, /device:TPU:1, one launch (start us, length us, event | category | flops | bytes accessed | tf_op | source)
XLA Modules:
  0.0 306.2 jit_solution(15842179457488552762)
XLA Ops:
  7.2 23.9 %all_to_all.45 = bf16[32,16,128]{2,1,0:T(8,128)(2,1)S(1)} all-to-all(bf16[32,16,128]{2,1,0:T(8,128)(2,1)} %bitcast.91), channel_id=1, replica_groups=mesh['seq'=32,'col'=8] {'seq'}, dimensions={0} | all-to-all | bytes 262144 | tf_op jit(solution)/shard_map/all_to_all | solution.py:59
  31.2 20.1 %all_to_all.46 = bf16[8,16,4096]{2,1,0:T(8,128)(2,1)S(1)} all-to-all(bf16[8,16,4096]{2,1,0:T(8,128)(2,1)S(1)} %broadcast_in_dim.5), channel_id=1, replica_groups=mesh['seq'=32,'col'=8] {'col'}, dimensions={0} | all-to-all | bytes 2097152 | tf_op jit(solution)/shard_map/all_to_all | solution.py:19
  51.4 2.0 convolution_convert_fusion.3
  54.8 53.9 %all-gather.2.cloned.1.call-done = bf16[4096,512]{1,0:T(8,128)(2,1)} async-done(((bf16[128,512]{1,0:T(8,128)(2,1)}), bf16[4096,512]{1,0:T(8,128)(2,1)}) %all-gather.2.cloned.1.call-update) | async-done | bytes 4194320 | tf_op jit(solution)/shard_map/all_gather | solution.py:34
  108.7 4.5 %fusion.19 = (bf16[4096,256]{1,0:T(8,128)(2,1)}, bf16[4096,256]{1,0:T(8,128)(2,1)}) fusion(bf16[4096,512]{1,0:T(8,128)(2,1)} %all-gather.2.cloned.1.call-done), kind=kLoop, calls=%fused_computation.31 | loop fusion | bytes 8388608 | tf_op jit(solution)/shard_map/split | solution.py:34
  113.2 4.1 %copy.43 = bf16[4096,256]{0,1:T(8,128)(2,1)} copy(bf16[4096,256]{1,0:T(8,128)(2,1)} %get-tuple-element.10) | data formatting | bytes 4194304 | tf_op jit(solution)/shard_map/split | solution.py:34
  117.3 4.1 %copy.41 = bf16[4096,256]{0,1:T(8,128)(2,1)} copy(bf16[4096,256]{1,0:T(8,128)(2,1)} %get-tuple-element.11) | data formatting | bytes 4194304 | tf_op jit(solution)/shard_map/split | solution.py:34
  121.5 10.1 %fusion.20 = (f32[4,256]{1,0:T(4,128)S(1)}, f32[4,256,4096]{1,2,0:T(8,128)}) fusion(bf16[4096,4,64]{0,2,1:T(8,128)(2,1)} %bitcast.79, bf16[256,4,64]{0,2,1:T(8,128)(2,1)S(1)} %bitcast.88), kind=kOutput, calls=%fused_computation.32 | convolution fusion | flops 549457920 | bytes 19009536 | tf_op jit(solution)/shard_map/sub | solution.py:79
  131.6 6.6 %fusion.9 = bf16[4,256,4096]{1,2,0:T(8,128)(2,1)S(1)} fusion(f32[4,256,4096]{1,2,0:T(8,128)} %get-tuple-element.13, f32[4,256]{1,0:T(4,128)S(1)} %get-tuple-element.12), kind=kLoop, calls=%fused_computation.11 | loop fusion | flops 8388608 | bytes 25169920 | tf_op jit(solution)/shard_map/convert_element_type | solution.py:81
  138.2 2.6 convolution_convert_fusion
  140.9 1.5 fusion.12
  142.4 7.6 %fusion.2 = bf16[4,256,4096]{1,2,0:T(8,128)(2,1)S(1)} fusion(bf16[4096,4,64]{0,2,1:T(8,128)(2,1)S(1)} %bitcast.78, bf16[256,4,64]{0,2,1:T(8,128)(2,1)S(1)} %bitcast.86, f32[4,256]{1,0:T(4,128)S(1)} %bitcast.92, f32[4,256,4096]{1,2,0:T(8,128)} %get-tuple-element.13, f32[4,256]{1,0:T(4,128)S(1)} %get-tuple-element.12), kind=kOutput, calls=%fused_computation.3 | convolution fusion | flops 557842432 | bytes 27402240 | tf_op jit(solution)/shard_map/qhd,khd->hqk/dot_general | solution.py:86
  150.0 2.6 convolution_convert_fusion.1
  153.2 2.4 pad_maximum_fusion
  155.6 6.5 %copy.55 = bf16[4096,512]{1,0:T(8,128)(2,1)} copy(bf16[4096,512]{0,1:T(8,128)(2,1)} %pad_maximum_fusion) | data formatting | bytes 8388608
  162.1 95.6 %reduce-scatter.4.cloned.1.call-done = bf16[128,512]{1,0:T(8,128)(2,1)} async-done(((bf16[4096,512]{1,0:T(8,128)(2,1)}), bf16[128,512]{1,0:T(8,128)(2,1)}) %reduce-scatter.4.cloned.1.call-update) | async-done | bytes 131088
  257.7 1.8 fusion.14
  259.5 0.8 fusion.10
  260.3 16.9 %all_to_all.47 = bf16[8,16,4096]{2,1,0:T(8,128)(2,1)S(1)} all-to-all(bf16[8,16,4096]{2,1,0:T(8,128)(2,1)S(1)} %bitcast.83), channel_id=1, replica_groups=mesh['seq'=32,'col'=8] {'col'}, dimensions={0} | all-to-all | bytes 2097152 | tf_op jit(solution)/shard_map/all_to_all | solution.py:53
  277.4 0.7 copy_bitcast_fusion.1
  278.0 9.8 %all-to-all-start.3 = ((bf16[16,32,128]{2,0,1:T(8,128)(2,1)}), bf16[16,32,128]{2,0,1:T(8,128)(2,1)S(1)}, u32[]{:S(2)}, u32[]{:S(2)}) async-start(bf16[16,32,128]{2,0,1:T(8,128)(2,1)} %copy_bitcast_fusion.1), calls=%async_computation.3 | async-start | bytes 262144 | tf_op jit(solution)/shard_map/all_to_all | solution.py:115
  287.9 5.5 %convolution_convert_fusion.2 = bf16[4,64,256]{2,1,0:T(8,128)(2,1)S(1)} fusion(bf16[4096,4,64]{0,2,1:T(8,128)(2,1)} %bitcast.80, bf16[4,256,4096]{1,2,0:T(8,128)(2,1)} %copy-done.1), kind=kOutput, calls=%fused_computation.19 | convolution fusion | flops 536936448 | bytes 10616832 | tf_op jit(solution)/shard_map/hqk,khd->qhd/dot_general | solution.py:90
  293.4 0.8 copy.50
  294.1 4.6 %all-to-all-done.3 = bf16[16,32,128]{2,0,1:T(8,128)(2,1)S(1)} async-done(((bf16[16,32,128]{2,0,1:T(8,128)(2,1)}), bf16[16,32,128]{2,0,1:T(8,128)(2,1)S(1)}, u32[]{:S(2)}, u32[]{:S(2)}) %all-to-all-start.3) | async-done | bytes 131104 | tf_op jit(solution)/shard_map/all_to_all | solution.py:115
  (26 shorter events, 2.9 us)
Async XLA Ops:
  7.2 46.2 %copy-start = (bf16[4096,256]{1,0:T(8,128)(2,1)S(1)}, bf16[4096,256]{1,0:T(8,128)(2,1)}, u32[]{:S(2)}) copy-start(bf16[4096,256]{1,0:T(8,128)(2,1)} %param.8) | copy-start | bytes 6291460
  7.2 101.6 %all-gather.2.cloned.1.call-start = ((), (), s32[]{:S(2)}) async-start(), calls=%async_computation.5 | async-start | bytes 4325376 | tf_op jit(solution)/shard_map/all_gather | solution.py:34
  31.2 23.4 %copy-start.5 = (bf16[256,256]{1,0:T(8,128)(2,1)S(1)}, bf16[256,256]{1,0:T(8,128)(2,1)}, u32[]{:S(2)}) copy-start(bf16[256,256]{1,0:T(8,128)(2,1)} %param.6) | copy-start | bytes 393220
  31.2 23.5 %copy-start.6 = (bf16[256,256]{1,0:T(8,128)(2,1)S(1)}, bf16[256,256]{1,0:T(8,128)(2,1)}, u32[]{:S(2)}) copy-start(bf16[256,256]{1,0:T(8,128)(2,1)} %param.7) | copy-start | bytes 393220
  54.5 203.1 %reduce-scatter.4.cloned.1.call-start = ((), (), s32[]{:S(2)}) async-start(), calls=%async_computation.6 | async-start | bytes 4325376
  138.2 2.6 copy-start.2
  149.9 3.2 %copy-start.1 = (bf16[4,256,4096]{1,2,0:T(8,128)(2,1)}, bf16[4,256,4096]{1,2,0:T(8,128)(2,1)S(1)}, u32[]{:S(2)}) copy-start(bf16[4,256,4096]{1,2,0:T(8,128)(2,1)S(1)} %fusion.2) | copy-start | bytes 25165828
  257.7 1.8 copy-start.3
  257.7 1.8 copy-start.4
  278.0 20.7 %all-to-all-start.3 = ((bf16[16,32,128]{2,0,1:T(8,128)(2,1)}), bf16[16,32,128]{2,0,1:T(8,128)(2,1)S(1)}, u32[]{:S(2)}, u32[]{:S(2)}) async-start(bf16[16,32,128]{2,0,1:T(8,128)(2,1)} %copy_bitcast_fusion.1), calls=%async_computation.3 | async-start | bytes 262144 | tf_op jit(solution)/shard_map/all_to_all | solution.py:115
Sparse Core Ops, SparseCore 0:
  54.7 54.0 all-gather.1
  162.2 95.3 reduce-scatter.3
where the time goes:
time: 307 us; the launch traced here: 306 us
  waiting for transfers between devices  154 us (50%)
  blocking collectives  60.9 us (20%)
  matrix products  35 us (11%)
  local copies, waits for them, and re-layouts  22.2 us (7%)
  between operations  14.2 us (5%)
  starting transfers between devices  9.9 us (3%)
  other arithmetic  9.88 us (3%)
    unnamed x3, waiting for transfers between devices  95.6 us
    all_gather x1, waiting for transfers between devices, in_one_piece(): lax.all_gather(both, axis, axis=dim, tiled=True)  53.9 us
    all_to_all x1, blocking collectives, local(): lax.all_to_all(memory, 'seq', split_axis=0, concat_axis=1, tiled=True)  23.9 us
    all_to_all x1, blocking collectives, sent_to_all(): lax.all_to_all(jnp.broadcast_to(array[None], (devices, *array.shape)), ax...  20.1 us
    all_to_all x1, blocking collectives, sum_at_owner(): lax.all_to_all(split_up(array, dim, devices), axis, 0, 0, tiled=True)  16.9 us
    split x3, local copies, waits for them, and re-layouts, in_one_piece(): jnp.split(lax.all_gather(both, axis, axis=dim, tiled=True), ends, axis=al...  12.7 us
    sub x1, matrix products, local(): expo = jnp.exp(scores - row_max)  10.1 us
    all_to_all x1, starting transfers between devices, local(): lax.all_to_all(summed, 'seq', split_axis=1, concat_axis=0, tiled=True)  9.82 us
  transfers between devices with their start and end apart: 3, of which 3 were waited for; matrix products, arithmetic and copies ran while one was open for 2% of the time, Pallas kernels for 0%

commit v1 on v0

v1 whole, which is shorter than its diff:
```python
import math

import jax
import jax.numpy as jnp
from jax import lax
from jax.experimental import pallas as pl
from jax.experimental.pallas import tpu as pltpu
from jax.sharding import PartitionSpec as P

HD = 64
BF = jnp.bfloat16
F32 = jnp.float32
MESH = pl.DeviceIdType.MESH
EXP2_SCALE = math.log2(math.e) / math.sqrt(HD)
FACTOR = 1.0 / math.sqrt(HD)


def mm(a, b):
    return jnp.dot(a, b, preferred_element_type=F32)


def roll64(a):
    return pltpu.roll(a, 64, 1)


def kernel(
    mem_hbm, q_hbm, g_hbm, wk_hbm, wv_hbm, dq_out, dm_out,
    wk, wv, wp, qin, gin, mem, kvl, kv, kvt, qgs, qg, qz, qt, gt, gz,
    sc, ex, ds, mx, ls, att, dlt, dqt, sb_s, sb_r, rs_s, rs_r, zb_s, zb, dq_s, dq_r,
    pm, em, fs, fo,
    in_sem, a_ss, a_rs, b_ss, b_rs, q_ss, q_rs, kz_ss, ky_ss, kf_ss, kb_ss, k_rs,
    sb_ss, sb_rs, r_ss, r_rs, z_ss, z_rs, d_ss, d_rs, e_ss, e_rs, f_ss, f_rs,
):
    s = lax.axis_index("seq")
    c = lax.axis_index("col")
    y, zh, j = s // 8, (s // 2) % 4, s % 2
    x, zl = c // 2, c % 2

    def at_seq(yy, zz, jj):
        return ((yy * 4 + zz) * 2 + jj, c)

    def send(src, dst, ss, rs, to):
        d = pltpu.make_async_remote_copy(
            src_ref=src, dst_ref=dst, send_sem=ss, recv_sem=rs,
            device_id=to, device_id_type=MESH,
        )
        d.start()
        return d

    def arrived(ref, rs):
        pltpu.make_async_remote_copy(
            src_ref=ref, dst_ref=ref, send_sem=rs, recv_sem=rs,
            device_id=(s, c), device_id_type=MESH,
        ).wait_recv()

    def sent(ref, ss):
        pltpu.make_async_remote_copy(
            src_ref=ref, dst_ref=ref, send_sem=ss, recv_sem=ss,
            device_id=(s, c), device_id_type=MESH,
        ).wait_send()

    barrier = pltpu.get_barrier_semaphore()

    @pl.loop(1, 32)
    def _(k):
        pl.semaphore_signal(barrier, inc=1, device_id=((s + k) % 32, c), device_id_type=MESH)

    @pl.loop(1, 8)
    def _(k):
        pl.semaphore_signal(barrier, inc=1, device_id=(s, (c + k) % 8), device_id_type=MESH)

    loads = [
        pltpu.make_async_copy(q_hbm, qin, in_sem.at[0]),
        pltpu.make_async_copy(g_hbm, gin, in_sem.at[1]),
        pltpu.make_async_copy(wk_hbm, wk, in_sem.at[2]),
        pltpu.make_async_copy(wv_hbm, wv, in_sem.at[3]),
        pltpu.make_async_copy(
            mem_hbm.at[s], mem.at[c, :, pl.ds(pl.multiple_of(s * 128, 128), 128)], in_sem.at[4]
        ),
    ]
    for ld in loads:
        ld.start()

    pl.semaphore_wait(barrier, 38)

    my_cols = pl.ds(pl.multiple_of(s * 128, 128), 128)

    @pl.loop(1, 32)
    def _(k):
        o = (s + k) % 32
        send(mem_hbm.at[o], mem.at[c, :, my_cols], a_ss.at[o], a_rs.at[s], (o, c))

    loads[0].wait()
    loads[1].wait()
    low = lax.broadcasted_iota(jnp.int32, (256, 128), 1) < HD
    for t in range(2):
        qtile = qin[:, t * 128 : (t + 1) * 128].astype(F32)
        gtile = gin[:, t * 128 : (t + 1) * 128].astype(F32)
        qgs[2 * t] = jnp.where(low, qtile, roll64(gtile)).astype(BF)
        qgs[2 * t + 1] = jnp.where(low, roll64(qtile), gtile).astype(BF)
    for k in (1, 3, 2):
        h = (zh + k) % 4
        send(qgs.at[h], qg.at[zh], q_ss.at[k], q_rs.at[zh], at_seq(y, h, j))
    qg[zh] = qgs[zh]

    loads[2].wait()
    loads[3].wait()
    low_w = lax.broadcasted_iota(jnp.int32, (256, 128), 1) < HD

    @pl.loop(0, 16)
    def _(i):
        rows = pl.ds(pl.multiple_of(i * 256, 256), 256)
        for t in range(2):
            kt = wk[rows, t * 128 : (t + 1) * 128].astype(F32)
            vt = wv[rows, t * 128 : (t + 1) * 128].astype(F32)
            wp[rows, 2 * t * 128 : (2 * t + 1) * 128] = jnp.where(low_w, kt, roll64(vt)).astype(BF)
            wp[rows, (2 * t + 1) * 128 : (2 * t + 2) * 128] = jnp.where(
                low_w, roll64(kt), vt
            ).astype(BF)

    loads[4].wait()

    @pl.loop(1, 32)
    def _(k):
        o = (s + k) % 32
        arrived(mem.at[c, :, pl.ds(pl.multiple_of(o * 128, 128), 128)], a_rs.at[o])

    def col(xx, zz):
        return xx * 2 + zz

    x1, x2, x3, ol = (x + 1) % 4, (x + 2) % 4, (x + 3) % 4, 1 - zl
    for n, to in enumerate((col(x, ol), col(x1, zl), col(x3, zl), col(x2, zl))):
        send(mem.at[c], mem.at[c], b_ss.at[n], b_rs.at[c], (s, to))
    p = col(x, ol)
    arrived(mem.at[p], b_rs.at[p])
    send(mem.at[p], mem.at[p], b_ss.at[4], b_rs.at[p], (s, col(x1, zl)))
    send(mem.at[p], mem.at[p], b_ss.at[5], b_rs.at[p], (s, col(x3, zl)))
    p2 = col(x2, zl)
    arrived(mem.at[p2], b_rs.at[p2])
    send(mem.at[p2], mem.at[p2], b_ss.at[6], b_rs.at[p2], (s, col(x, ol)))
    for p in (col(x1, zl), col(x3, zl), col(x1, ol), col(x3, ol), col(x2, ol)):
        arrived(mem.at[p], b_rs.at[p])

    rows_all = mem[...].reshape(128, 4096)
    kv_new = mm(rows_all, wp[...]).astype(BF)
    for h in range(4):
        kvl[h] = kv_new[:, h * 128 : (h + 1) * 128]

    def slot(jj, yy, zz):
        return kv.at[jj * 4 + yy, pl.ds(pl.multiple_of(zz * 128, 128), 128)]

    def slot_sem(jj, yy, zz):
        return k_rs.at[(jj * 4 + yy) * 4 + zz]

    for k in (1, 3, 2):
        h = (zh + k) % 4
        send(kvl.at[h], slot(j, y, zh), kz_ss.at[k], slot_sem(j, y, zh), at_seq(y, h, j))
    slot(j, y, zh)[...] = kvl[zh]
    y1, y2, y3, oj = (y + 1) % 4, (y + 2) % 4, (y + 3) % 4, 1 - j

    def share(yy, zz, sem, to):
        send(slot(j, yy, zz), slot(j, yy, zz), sem, slot_sem(j, yy, zz), to)

    for k in (0, 1, 3, 2):
        zz = (zh + k) % 4
        if k:
            arrived(slot(j, y, zz), slot_sem(j, y, zz))
        share(y, zz, ky_ss.at[0, k], at_seq(y1, zh, j))
        share(y, zz, ky_ss.at[1, k], at_seq(y3, zh, j))
        share(y, zz, kb_ss.at[0, k], at_seq(y, zh, oj))

    low_q = lax.broadcasted_iota(jnp.int32, (256, 128), 1) < HD
    low_t = lax.broadcasted_iota(jnp.int32, (128, 256), 0) < HD
    for k in (0, 1, 3, 2):
        b = (zh + k) % 4
        if k:
            arrived(qg.at[b], q_rs.at[b])
    for b in range(4):
        both = qg[b].astype(F32)
        qz[b] = jnp.where(low_q, both, 0.0).astype(BF)
        turned = both.T
        qt[:, b * 256 : (b + 1) * 256] = jnp.where(low_t, turned, 0.0).astype(BF)
        gt[:, b * 256 : (b + 1) * 256] = jnp.where(low_t, 0.0, turned)
    mx[...] = jnp.full((8, 1024), -jnp.inf, F32)

    def scores(ch):
        for r in range(2):
            part = kv[ch, r * 256 : (r + 1) * 256, :]
            kvt[ch, :, r * 256 : (r + 1) * 256] = part.astype(F32).T.astype(BF)
            for b in range(4):
                cols = slice(b * 256, (b + 1) * 256)
                v = mm(part, qt[:, cols])
                sc[ch, r * 256 : (r + 1) * 256, cols] = v
                mx[:, cols] = jnp.maximum(mx[:, cols], v.reshape(32, 8, 256).max(axis=0))

    scores(j * 4 + y)
    for zz in range(4):
        arrived(slot(j, y3, zz), slot_sem(j, y3, zz))
        share(y3, zz, kb_ss.at[1, zz], at_seq(y, zh, oj))
        if zz < 2:
            share(y3, zz, kf_ss.at[zz], at_seq(y1, zh, j))
        arrived(slot(j, y1, zz), slot_sem(j, y1, zz))
        share(y1, zz, kb_ss.at[2, zz], at_seq(y, zh, oj))
        if zz >= 2:
            share(y1, zz, kf_ss.at[zz], at_seq(y3, zh, j))
    for zz in range(4):
        arrived(slot(j, y2, zz), slot_sem(j, y2, zz))
        share(y2, zz, kb_ss.at[3, zz], at_seq(y, zh, oj))

    @pl.loop(1, 4)
    def _(k):
        scores(j * 4 + (y + k) % 4)

    @pl.loop(0, 16)
    def _(i):
        zz, yy = i % 4, i // 4
        arrived(slot(oj, yy, zz), slot_sem(oj, yy, zz))

    @pl.loop(0, 4)
    def _(k):
        scores(oj * 4 + k)

    mx[...] = jnp.broadcast_to(jnp.max(mx[...], axis=0, keepdims=True), (8, 1024))
    ls[...] = jnp.zeros((8, 1024), F32)
    att[...] = jnp.zeros((128, 1024), F32)

    @pl.loop(0, 8)
    def _(ch):
        for b in range(4):
            cols = slice(b * 256, (b + 1) * 256)
            top = mx[0:1, cols]
            total = jnp.zeros((8, 256), F32)
            for r in range(2):
                rows = slice(r * 256, (r + 1) * 256)
                e = jnp.exp2((sc[ch, rows, cols] - top) * EXP2_SCALE)
                total = total + e.reshape(32, 8, 256).sum(axis=0)
                ex[ch, rows, cols] = e.astype(BF)
            ls[:, cols] += total
            att[:, cols] += mm(kvt[ch], ex[ch, :, cols])

    for b in range(4):
        cols = slice(b * 256, (b + 1) * 256)
        inv = 1.0 / jnp.sum(ls[:, cols], axis=0, keepdims=True)
        scaled = (gt[:, cols] * inv).astype(BF)
        wide = scaled.astype(F32)
        gt[:, cols] = wide
        gz[b] = wide.T.astype(BF)
        dlt[:, cols] = jnp.broadcast_to(
            jnp.sum(wide * (att[:, cols] * inv), axis=0, keepdims=True), (8, 256)
        )
        qt[:, cols] = scaled
    dqt[...] = jnp.zeros((128, 1024), F32)
    low_o = lax.broadcasted_iota(jnp.int32, (512, 128), 1) < HD

    def grads(ch):
        for b in range(4):
            cols = slice(b * 256, (b + 1) * 256)
            delta = dlt[0:1, cols]
            for r in range(2):
                rows = slice(r * 256, (r + 1) * 256)
                pg = mm(kv[ch, rows, :], qt[:, cols])
                ds[rows, cols] = (ex[ch, rows, cols].astype(F32) * (pg - delta)).astype(BF)
            dqt[:, cols] += mm(kvt[ch], ds[:, cols])
        qall = qz[...].reshape(1024, 128)
        gall = gz[...].reshape(1024, 128)
        dk = mm(ds[...], qall)
        dv = mm(ex[ch], gall)
        return jnp.where(low_o, dk * FACTOR, dv)

    @pl.loop(0, 4)
    def _(k):
        yy = (y + 2 + k) % 4
        sb_s[k] = grads(oj * 4 + yy).astype(BF)
        send(sb_s.at[k], sb_r.at[k], sb_ss.at[k], sb_rs.at[k], at_seq(y, zh, oj))

    @pl.loop(0, 3)
    def _(k):
        yy = (y + 2 + k + k // 2) % 4
        mine = grads(j * 4 + yy)
        at = k + k // 2
        arrived(sb_r.at[at], sb_rs.at[at])
        rs_s[k] = (mine + sb_r[at].astype(F32)).astype(BF)
        send(rs_s.at[k], rs_r.at[k], r_ss.at[k], r_rs.at[k], at_seq(yy, zh, j))

    total = grads(j * 4 + y)
    arrived(sb_r.at[2], sb_rs.at[2])
    total = total + sb_r[2].astype(F32)
    for k in range(3):
        arrived(rs_r.at[k], r_rs.at[k])
        total = total + rs_r[k].astype(F32)
    zb_s[...] = total.astype(BF).reshape(4, 128, 128)
    head_cols = pl.ds(pl.multiple_of(zh * 128, 128), 128)
    for k in (1, 3, 2):
        zz = (zh + k) % 4
        send(zb_s.at[zz], zb.at[:, head_cols], z_ss.at[k], z_rs.at[zh], at_seq(y, zz, j))
    zb[:, head_cols] = zb_s[zh]

    low_d = lax.broadcasted_iota(jnp.int32, (128, 128), 1) < HD
    for b in range(4):
        back = (dqt[:, b * 256 : (b + 1) * 256] * FACTOR).T
        dq_s[b] = jnp.where(low_d, back[:128], roll64(back[128:])).astype(BF)
    for k in (1, 3, 2):
        zz = (zh + k) % 4
        send(dq_s.at[zz], dq_r.at[zh], d_ss.at[k], d_rs.at[zh], at_seq(y, zz, j))
    dq_r[zh] = dq_s[zh]

    for k in (1, 3, 2):
        zz = (zh + k) % 4
        arrived(zb.at[:, pl.ds(pl.multiple_of(zz * 128, 128), 128)], z_rs.at[zz])
    lhs = zb[...]
    for n in range(8):
        part = lax.dot_general(
            lhs, wp[n * 512 : (n + 1) * 512, :], (((1,), (1,)), ((), ())),
            preferred_element_type=F32,
        ).astype(BF)
        pm[:, :, n * 512 : (n + 1) * 512] = part.reshape(8, 16, 512)
    for k in (4, 1, 7, 2, 6, 3, 5):
        o = (c + k) % 8
        send(pm.at[o], em.at[c], e_ss.at[k], e_rs.at[c], (s, o))

    for k in (1, 3, 2):
        zz = (zh + k) % 4
        arrived(dq_r.at[zz], d_rs.at[zz])
    for t in range(2):
        a = dq_r[2 * t].astype(F32)
        b = dq_r[2 * t + 1].astype(F32)
        tile = slice(t * 128, (t + 1) * 128)
        dq_out[0:128, tile] = jnp.where(low_d, a, roll64(b)).astype(BF)
        dq_out[128:256, tile] = jnp.where(low_d, roll64(a), b).astype(BF)

    em[c] = pm[c]
    for k in range(1, 8):
        o = (c + k) % 8
        arrived(em.at[o], e_rs.at[o])
    acc = em[0].astype(F32)
    for k in range(1, 8):
        acc = acc + em[k].astype(F32)
    fs[...] = acc.astype(BF)

    @pl.loop(1, 32)
    def _(k):
        o = (s + k) % 32
        send(
            fs.at[:, pl.ds(pl.multiple_of(o * 128, 128), 128)], fo.at[s],
            f_ss.at[o], f_rs.at[s], (o, c),
        )

    fo[s] = fs[:, my_cols]

    @pl.loop(1, 32)
    def _(k):
        o = (s + k) % 32
        arrived(fo.at[o], f_rs.at[o])

    dm_out[...] = fo[...]

    @pl.loop(1, 32)
    def _(k):
        o = (s + k) % 32
        sent(fo.at[o], a_ss.at[o])
        sent(fo.at[o], f_ss.at[o])

    for n in range(7):
        sent(mem.at[0], b_ss.at[n])
        sent(pm.at[0], e_ss.at[n + 1])
    for k in range(1, 4):
        sent(qgs.at[0], q_ss.at[k])
        sent(kvl.at[0], kz_ss.at[k])
        sent(zb_s.at[0], z_ss.at[k])
        sent(dq_s.at[0], d_ss.at[k])
        sent(rs_s.at[0], r_ss.at[k - 1])
    for k in range(4):
        sent(kvl.at[0], ky_ss.at[0, k])
        sent(kvl.at[0], ky_ss.at[1, k])
        sent(kvl.at[0], kf_ss.at[k])
        sent(sb_s.at[0], sb_ss.at[k])
        for n in range(4):
            sent(kvl.at[0], kb_ss.at[n, k])


def local(memory, query, out_grad, w_key, w_value):
    dma = pltpu.SemaphoreType.DMA
    v = pltpu.VMEM
    dq, dm = pl.pallas_call(
        kernel,
        out_shape=(
            jax.ShapeDtypeStruct((256, 256), BF),
            jax.ShapeDtypeStruct((32, 16, 128), BF),
        ),
        in_specs=[pl.BlockSpec(memory_space=pl.ANY)] * 5,
        out_specs=(pl.BlockSpec(memory_space=pltpu.VMEM),) * 2,
        scratch_shapes=[
            v((4096, 256), BF), v((4096, 256), BF), v((4096, 512), BF),
            v((256, 256), BF), v((256, 256), BF),
            v((8, 16, 4096), BF), v((4, 128, 128), BF),
            v((8, 512, 128), BF), v((8, 128, 512), BF),
            v((4, 256, 128), BF), v((4, 256, 128), BF), v((4, 256, 128), BF),
            v((128, 1024), BF), v((128, 1024), F32), v((4, 256, 128), BF),
            v((8, 512, 1024), F32), v((8, 512, 1024), BF), v((512, 1024), BF),
            v((8, 1024), F32), v((8, 1024), F32), v((128, 1024), F32), v((8, 1024), F32),
            v((128, 1024), F32),
            v((4, 512, 128), BF), v((4, 512, 128), BF),
            v((3, 512, 128), BF), v((3, 512, 128), BF),
            v((4, 128, 128), BF), v((128, 512), BF),
            v((4, 128, 128), BF), v((4, 128, 128), BF),
            v((8, 16, 4096), BF), v((8, 16, 4096), BF),
            v((16, 4096), BF), v((32, 16, 128), BF),
            dma((5,)), dma((32,)), dma((32,)), dma((7,)), dma((8,)),
            dma((4,)), dma((4,)), dma((4,)), dma((2, 4)), dma((4,)), dma((4, 4)), dma((32,)),
            dma((4,)), dma((4,)), dma((3,)), dma((3,)), dma((4,)), dma((4,)),
            dma((4,)), dma((4,)), dma((8,)), dma((8,)), dma((32,)), dma((32,)),
        ],
        compiler_params=pltpu.CompilerParams(
            collective_id=0, has_side_effects=True, vmem_limit_bytes=60 * 1024 * 1024
        ),
    )(memory.reshape(32, 16, 128), query, out_grad, w_key, w_value)
    return dq, dm.reshape(512, 128)


def solution(mesh):
    return jax.shard_map(
        local,
        mesh=mesh,
        in_specs=(
            P("col", "seq"),
            P("seq", "col"),
            P("seq", "col"),
            P(None, "col"),
            P(None, "col"),
        ),
        out_specs=(P("seq", "col"), P("col", "seq")),
        check_vma=False,
    )
```

time: 307 us -> 106 us (0.35)
  waiting for transfers between devices: 154 us -> 0 us
  Pallas kernels: 0 us -> 102 us
  blocking collectives: 60.9 us -> 0 us
  matrix products: 35 us -> 0 us
  local copies, waits for them, and re-layouts: 22.2 us -> 3.14 us
  between operations: 14.2 us -> 0.64 us
  starting transfers between devices: 9.9 us -> 0 us
  other arithmetic: 9.88 us -> 0 us
    pallas_call x0 -> x1, Pallas kernels: none -> 102 us  [local(): pl.pallas_call(kernel, out_shape=(jax.ShapeDtypeStruct((256, 256), BF), j...]
    unnamed x3 -> x0, waiting for transfers between devices: 95.6 us -> none
    all_to_all x3 -> x0, blocking collectives: 60.9 us -> none  [the longest x1 23.9 us: local(): lax.all_to_all(memory, 'seq', split_axis=0, concat_axis=1, tiled=True)]
    all_gather x1 -> x0, waiting for transfers between devices: 53.9 us -> none  [in_one_piece(): lax.all_gather(both, axis, axis=dim, tiled=True)]
    dot_general x9 -> x0, matrix products: 24.9 us -> none  [the longest x1 7.55 us: local(): jnp.einsum('qhd,khd->hqk', grad_heads, value_heads, preferred_element_typ...]
    split x3 -> x0, local copies, waits for them, and re-layouts: 12.7 us -> none  [in_one_piece(): jnp.split(lax.all_gather(both, axis, axis=dim, tiled=True), ends, axis=al...]
    sub x1 -> x0, matrix products: 10.1 us -> none  [local(): expo = jnp.exp(scores - row_max)]
    all_to_all x1 -> x0, starting transfers between devices: 9.82 us -> none  [local(): lax.all_to_all(summed, 'seq', split_axis=1, concat_axis=0, tiled=True)]
  transfers between devices with their start and end apart: 3 -> 0, of which waited for: 3 -> 0; matrix products, arithmetic and copies ran while one was open for 2% -> 0% of each run, Pallas kernels for 0% -> 0%
where the time goes in v1:
time: 106 us
  Pallas kernels  102 us (96%)
  local copies, waits for them, and re-layouts  3.14 us (3%)
    pallas_call x1, Pallas kernels, local(): pl.pallas_call(kernel, out_shape=(jax.ShapeDtypeStruct((256, 256), BF), j...  102 us
    unnamed x2, local copies, waits for them, and re-layouts  3.14 us

profile of v1, /device:TPU:1, one launch (start us, length us, event | category | flops | bytes accessed | tf_op | source)
XLA Modules:
  0.0 105.7 jit_solution(2436336069460311841)
XLA Ops:
  0.6 101.9 %shard_map.68 = (bf16[256,256]{1,0:T(8,128)(2,1)}, bf16[32,16,128]{2,1,0:T(8,128)(2,1)}) custom-call(bf16[32,16,128]{2,1,0:T(8,128)(2,1)} %bitcast.2, bf16[256,256]{1,0:T(8,128)(2,1)} %q_hbm.1, bf16[256,256]{1,0:T(8,128)(2,1)} %g_hbm.1, bf16[4096,256]{1,0:T(8,128)(2,1)} %wk_hbm.1, bf16[4096,256]{1,0:T(8,128)(2,1)} %wv_hbm.1), custom_call_target="tpu_custom_call" | custom-call | tf_op jit(solution)/shard_map/pallas_call | solution.py:384
  102.6 1.6 %copy.9 = bf16[256,256]{1,0:T(8,128)(2,1)} copy(bf16[256,256]{1,0:T(8,128)(2,1)} %get-tuple-element.8) | data formatting | bytes 262144
  104.1 1.6 %copy.10 = bf16[512,128]{1,0:T(8,128)(2,1)} copy(bf16[512,128]{1,0:T(8,128)(2,1)} %bitcast.3) | data formatting | bytes 262144

commit v2 on v0

v2 whole, which is shorter than its diff:
```python
import math

import jax
import jax.numpy as jnp
from jax import lax
from jax.experimental import pallas as pl
from jax.experimental.pallas import tpu as pltpu
from jax.sharding import PartitionSpec as P

HD = 64
BF = jnp.bfloat16
F32 = jnp.float32
MESH = pl.DeviceIdType.MESH
EXP2_SCALE = math.log2(math.e) / math.sqrt(HD)
FACTOR = 1.0 / math.sqrt(HD)


def mm(a, b):
    return jnp.dot(a, b, preferred_element_type=F32)


def mm_t(a, b):
    return lax.dot_general(a, b, (((1,), (1,)), ((), ())), preferred_element_type=F32)


def roll64(a):
    return pltpu.roll(a, 64, 1)


def kernel(
    mem_hbm, q_hbm, g_hbm, wk_hbm, wv_hbm, dq_out, dm_out,
    wk, wv, wp, qin, gin, mem, kvl, kv, kvt, q_s, q_r, g_s, g_r, qt, gt, gs,
    sc, ex, ds, mx, tops, ls, att, dqt, gk, sb_s, sb_r, rs_s, rs_r, tot, zb_s, zb, dq_s, dq_r,
    pm, e1_r, e2_s, e2_r, fs, fo,
    in_sem, ss, a_rs, b_rs, k_rs, sb_rs, r_rs, d_rs, e_rs,
):
    s = lax.axis_index("seq")
    c = lax.axis_index("col")
    y, zh, j = s // 8, (s // 2) % 4, s % 2
    x, zl = c // 2, c % 2

    def at_seq(yy, zz, jj):
        return ((yy * 4 + zz) * 2 + jj, c)

    def send(src, dst, ss, rs, to):
        d = pltpu.make_async_remote_copy(
            src_ref=src, dst_ref=dst, send_sem=ss, recv_sem=rs,
            device_id=to, device_id_type=MESH,
        )
        d.start()
        return d

    def arrived(ref, rs):
        pltpu.make_async_remote_copy(
            src_ref=ref, dst_ref=ref, send_sem=rs, recv_sem=rs,
            device_id=(s, c), device_id_type=MESH,
        ).wait_recv()

    def sent(ref, ss):
        pltpu.make_async_remote_copy(
            src_ref=ref, dst_ref=ref, send_sem=ss, recv_sem=ss,
            device_id=(s, c), device_id_type=MESH,
        ).wait_send()

    barrier = pltpu.get_barrier_semaphore()

    @pl.loop(1, 32)
    def _(k):
        pl.semaphore_signal(barrier, inc=1, device_id=((s + k) % 32, c), device_id_type=MESH)

    @pl.loop(1, 8)
    def _(k):
        pl.semaphore_signal(barrier, inc=1, device_id=(s, (c + k) % 8), device_id_type=MESH)

    loads = [
        pltpu.make_async_copy(q_hbm, qin, in_sem.at[0]),
        pltpu.make_async_copy(g_hbm, gin, in_sem.at[1]),
        pltpu.make_async_copy(wk_hbm, wk, in_sem.at[2]),
        pltpu.make_async_copy(wv_hbm, wv, in_sem.at[3]),
        pltpu.make_async_copy(
            mem_hbm.at[s],
            mem.at[zh, c, :, pl.ds(pl.multiple_of((y * 2 + j) * 128, 128), 128)],
            in_sem.at[4],
        ),
    ]
    for ld in loads:
        ld.start()

    pl.semaphore_wait(barrier, 38)

    my_cols = pl.ds(pl.multiple_of((y * 2 + j) * 128, 128), 128)
    near = (0, 1, 3, 2)

    def feature_group(dz, act):
        @pl.loop(0 if dz else 1, 8)
        def _(m):
            oy, oc = (y + m // 2) % 4, (j + m) % 2
            cols = pl.ds(pl.multiple_of((oy * 2 + oc) * 128, 128), 128)
            act((oy * 4 + (zh + dz) % 4) * 2 + oc, cols)

    back = (0, 2, 1, 3)
    for n, dz in enumerate(near):
        feature_group(
            dz,
            lambda o, cols: send(
                mem_hbm.at[o], mem.at[zh, c, :, my_cols], ss.at[0], a_rs.at[back[n]], (o, c)
            ),
        )

    low = lax.broadcasted_iota(jnp.int32, (128, 128), 1) < HD

    def halves(top, bottom):
        return (
            jnp.where(low, top, roll64(bottom)).astype(BF),
            jnp.where(low, roll64(top), bottom).astype(BF),
        )

    def pack_heads(rows, out):
        for t in range(2):
            tile = slice(t * 128, (t + 1) * 128)
            out[2 * t], out[2 * t + 1] = halves(
                rows[0:128, tile].astype(F32), rows[128:256, tile].astype(F32)
            )

    def deal(out, into, which):
        for k in (1, 3, 2):
            h = (zh + k) % 4
            send(out.at[h], into.at[zh], ss.at[which], d_rs.at[which], at_seq(y, h, j))
        into[zh] = out[zh]

    def dealt(into, which):
        arrived(into.at[pl.ds(0, 3)], d_rs.at[which])

    loads[0].wait()
    loads[1].wait()
    pack_heads(qin, q_s)
    pack_heads(gin, g_s)

    loads[2].wait()
    loads[3].wait()
    low_w = lax.broadcasted_iota(jnp.int32, (256, 128), 1) < HD

    @pl.loop(0, 16)
    def _(i):
        rows = pl.ds(pl.multiple_of(i * 256, 256), 256)
        sub = pl.ds(pl.multiple_of(i // 4 * 256, 256), 256)
        for t in range(2):
            kt = wk[rows, t * 128 : (t + 1) * 128].astype(F32)
            vt = wv[rows, t * 128 : (t + 1) * 128].astype(F32)
            wp[i % 4, sub, 2 * t * 128 : (2 * t + 1) * 128] = jnp.where(low_w, kt, roll64(vt)).astype(BF)
            wp[i % 4, sub, (2 * t + 1) * 128 : (2 * t + 2) * 128] = jnp.where(
                low_w, roll64(kt), vt
            ).astype(BF)

    loads[4].wait()

    def col(xx, zz):
        return xx * 2 + zz

    x1, x2, x3, ol = (x + 1) % 4, (x + 2) % 4, (x + 3) % 4, 1 - zl

    def quarter(n):
        return (zh + near[n]) % 4

    def pass_on(p, n, which, to):
        here = mem.at[quarter(n), p]
        send(here, here, ss.at[4], b_rs.at[n, which], (s, to))

    def own_rows(n):
        if n:
            arrived(mem.at[quarter(n), c], a_rs.at[n])
        else:
            arrived(fo.at[pl.ds(0, 7)], a_rs.at[n])
        pass_on(c, n, 2, col(x1, zl))
        pass_on(c, n, 2, col(x3, zl))
        pass_on(c, n, 0, col(x, ol))
        pass_on(c, n, 1, col(x2, zl))

    def relay_near(n):
        arrived(mem.at[quarter(n), 0], b_rs.at[n, 0])
        pass_on(col(x, ol), n, 2, col(x1, zl))
        pass_on(col(x, ol), n, 2, col(x3, zl))

    def relay_far(n):
        arrived(mem.at[quarter(n), 0], b_rs.at[n, 1])
        pass_on(col(x2, zl), n, 2, col(x, ol))

    own_rows(0)
    own_rows(1)
    relay_near(0)
    own_rows(2)
    relay_near(1)
    own_rows(3)
    deal(q_s, q_r, 1)
    relay_far(0)
    relay_near(2)
    relay_far(1)
    relay_near(3)
    relay_far(2)
    relay_far(3)

    kv_new = jnp.zeros((128, 512), F32)
    for n in range(4):
        arrived(mem.at[quarter(n), pl.ds(0, 5)], b_rs.at[n, 2])
        kv_new = kv_new + mm(mem[quarter(n)].reshape(128, 1024), wp[quarter(n)])
    kv_new = kv_new.astype(BF)
    for h in range(4):
        kvl[h] = kv_new[:, h * 128 : (h + 1) * 128]

    def slot(jj, yy, zz):
        return kv.at[jj * 4 + yy, pl.ds(pl.multiple_of(zz * 128, 128), 128)]

    for k in (1, 3, 2):
        h = (zh + k) % 4
        send(kvl.at[h], slot(j, y, zh), ss.at[12], k_rs.at[4 - k], at_seq(y, h, j))
    slot(j, y, zh)[...] = kvl[zh]
    deal(g_s, g_r, 2)
    y1, y2, y3, oj = (y + 1) % 4, (y + 2) % 4, (y + 3) % 4, 1 - j

    def share(yy, zz, sem, to):
        send(slot(j, yy, zz), slot(j, yy, zz), ss.at[5], k_rs.at[sem], to)

    for n, k in enumerate(near):
        zz = (zh + k) % 4
        if k:
            arrived(slot(j, y, zz), k_rs.at[k])
        share(y, zz, 4 + n, at_seq(y1, zh, j))
        share(y, zz, 8 + n, at_seq(y3, zh, j))
        share(y, zz, 13, at_seq(y, zh, oj))

    qt[HD:, :] = jnp.zeros((HD, 1024), BF)
    dealt(q_r, 1)
    for b in range(4):
        turned = q_r[b].astype(F32).T.astype(BF)
        qt[0:HD, b * 256 : b * 256 + 128] = turned[:HD]
        qt[0:HD, b * 256 + 128 : (b + 1) * 256] = turned[HD:]
    mx[...] = jnp.full((8, 1024), -jnp.inf, F32)
    ls[...] = jnp.zeros((8, 1024), F32)
    att[...] = jnp.zeros((HD, 1024), F32)

    def stage(body):
        @pl.loop(0, 1)
        def _(_):
            for b in range(4):
                body(slice(b * 256, (b + 1) * 256))

    def attend(ch):
        def score(cols):
            top = jnp.full((8, 256), -jnp.inf, F32)
            for r in range(2):
                rows = slice(r * 256, (r + 1) * 256)
                v = mm(kv[ch, rows, :], qt[:, cols])
                sc[rows, cols] = v
                top = jnp.maximum(top, v.reshape(32, 8, 256).max(axis=0))
            top = jnp.maximum(mx[0:1, cols], jnp.max(top, axis=0, keepdims=True))
            tops[ch, :, cols] = jnp.broadcast_to(top, (8, 256))

        def weigh(cols):
            top = tops[ch, 0:1, cols]
            shrink = jnp.exp2((mx[0:1, cols] - top) * EXP2_SCALE)
            mx[:, cols] = tops[ch, :, cols]
            total = ls[:, cols] * shrink
            for r in range(2):
                rows = slice(r * 256, (r + 1) * 256)
                e = jnp.exp2((sc[rows, cols] - top) * EXP2_SCALE)
                total = total + e.reshape(32, 8, 256).sum(axis=0)
                ex[ch, rows, cols] = e.astype(BF)
            ls[:, cols] = total
            att[:, cols] = att[:, cols] * shrink + mm(kvt[ch, HD:, :], ex[ch, :, cols])

        for r in range(2):
            rows = slice(r * 256, (r + 1) * 256)
            kvt[ch, :, rows] = kv[ch, rows, :].astype(F32).T.astype(BF)
        stage(score)
        stage(weigh)

    attend(j * 4 + y)
    for n, k in enumerate(near):
        zz = (zh + k) % 4
        arrived(slot(j, y3, zz), k_rs.at[4 + n])
        if n < 2:
            share(y3, zz, 12, at_seq(y1, zh, j))
        share(y3, zz, 16, at_seq(y, zh, oj))
        arrived(slot(j, y1, zz), k_rs.at[8 + n])
        if n >= 2:
            share(y1, zz, 12, at_seq(y3, zh, j))
        share(y1, zz, 14, at_seq(y, zh, oj))

    @pl.loop(0, 7)
    def _(i):
        k = jnp.where(i == 0, 3, jnp.where(i == 1, 1, jnp.where(i == 2, 2, 0)))
        k = jnp.where(i < 3, k, jnp.where(i == 4, 3, jnp.where(i == 5, 1, jnp.where(i == 6, 2, k))))
        yy = (y + k) % 4

        @pl.when(i == 1)
        def _():
            far = kv.at[j * 4 + y2]
            arrived(far, k_rs.at[12])
            send(far, far, ss.at[5], k_rs.at[15], at_seq(y, zh, oj))

        @pl.when(i >= 3)
        def _():
            arrived(kv.at[oj * 4 + yy], k_rs.at[13 + k])

        attend(jnp.where(i < 3, j, oj) * 4 + yy)

    dealt(g_r, 2)
    gs[0:HD, :] = jnp.zeros((HD, 1024), BF)
    for b in range(4):
        cols = slice(b * 256, (b + 1) * 256)
        turned = g_r[b].astype(F32).T
        inv = 1.0 / jnp.sum(ls[:, cols], axis=0, keepdims=True)
        gt[:, b * 256 : b * 256 + 128] = turned[:HD] * inv[:, :128]
        gt[:, b * 256 + 128 : (b + 1) * 256] = turned[HD:] * inv[:, 128:]
        att[:, cols] = att[:, cols] * inv
    dqt[...] = jnp.zeros((HD, 1024), F32)

    def grads(ch):
        def score_grad(cols):
            shrink = jnp.exp2((tops[ch, 0:1, cols] - mx[0:1, cols]) * EXP2_SCALE)
            scaled = (gt[:, cols] * shrink).astype(BF)
            gs[HD:, cols] = scaled
            delta = jnp.sum(scaled.astype(F32) * att[:, cols], axis=0, keepdims=True)
            for r in range(2):
                rows = slice(r * 256, (r + 1) * 256)
                pg = mm(kv[ch, rows, :], gs[:, cols])
                ds[rows, cols] = (ex[ch, rows, cols].astype(F32) * (pg - delta)).astype(BF)

        def query_grad(cols):
            dqt[:, cols] += mm(kvt[ch, 0:HD, :], ds[:, cols])

        stage(score_grad)
        stage(query_grad)
        dk = mm_t(qt[0:HD, :], ds[...]) * FACTOR
        dv = mm_t(gs[HD:, :], ex[ch])
        for zz in range(4):
            gk[zz, 0:HD, :] = dk[:, zz * 128 : (zz + 1) * 128]
            gk[zz, HD:, :] = dv[:, zz * 128 : (zz + 1) * 128]

    at_kz = tuple((zh + k) % 4 for k in (1, 3, 2, 0))

    @pl.loop(0, 8)
    def _(i):
        mine = (i == 2) | (i == 4) | (i == 5) | (i == 7)
        far = jnp.where(i < 4, jnp.where(i == 3, 3, jnp.where(i == 1, 1, 0)), 2)
        k = jnp.where(i == 4, 1, jnp.where(i == 5, 3, far))
        yy = (y + 2 + k) % 4
        grads(jnp.where(mine, j, oj) * 4 + yy)

        @pl.when(jnp.logical_not(mine))
        def _():
            sb_s[k] = gk[...].astype(BF)
            send(sb_s.at[k], sb_r.at[k], ss.at[6], sb_rs.at[k], at_seq(y, zh, oj))

        @pl.when(mine)
        def _():
            arrived(sb_r.at[k], sb_rs.at[k])
            both = gk[...] + sb_r[k].astype(F32)

            @pl.when(k == 2)
            def _():
                tot[...] = both

            @pl.when(k != 2)
            def _():
                at = k - k // 3
                rs_s[at] = both.astype(BF)
                for n, zz in enumerate(at_kz):
                    send(
                        rs_s.at[at, zz], rs_r.at[at, zz], ss.at[11], r_rs.at[n],
                        at_seq(yy, zh, j),
                    )

    for b in range(4):
        pair = [dqt[:, b * 256 + r * 128 : b * 256 + (r + 1) * 128] * FACTOR for r in range(2)]
        dq_s[b] = jnp.concatenate(pair, axis=0).T.astype(BF)

    head_cols = pl.ds(pl.multiple_of(zh * 128, 128), 128)
    for n, zz in enumerate(at_kz):
        acc = tot[zz]
        arrived(rs_r.at[pl.ds(0, 3), 0], r_rs.at[n])
        for k in range(3):
            acc = acc + rs_r[k, zz].astype(F32)
        acc = acc.T
        if n < 3:
            zb_s[zz] = acc.astype(BF)
            send(zb_s.at[zz], zb.at[:, head_cols], ss.at[7], d_rs.at[0], at_seq(y, zz, j))
        else:
            zb[:, head_cols] = acc.astype(BF)

    arrived(zb.at[:, pl.ds(0, 384)], d_rs.at[0])
    lhs = zb[...]
    far_first = (2, 3, 1, 0)

    def partial(n):
        zq = (zh + far_first[n]) % 4
        for r in range(2):
            part = mm_t(lhs, wp[zq, r * 512 : (r + 1) * 512, :]).astype(BF)
            pm[n, :, :, r * 512 : (r + 1) * 512] = part.reshape(8, 16, 512)
        for i, (block, to) in enumerate((
            (col(x2, ol), col(x, ol)),
            (col(x1, ol), col(x1, zl)),
            (col(x3, ol), col(x3, zl)),
            (col(x1, zl), col(x1, zl)),
            (col(x3, zl), col(x3, zl)),
        )):
            send(pm.at[n, block], e1_r.at[n, i], ss.at[8], e_rs.at[n, (i + 1) // 2], (s, to))

    def combine(n):
        arrived(e1_r.at[n, 0], e_rs.at[n, 0])
        e2_s[n, 0] = (e1_r[n, 0].astype(F32) + pm[n, col(x2, zl)].astype(F32)).astype(BF)
        send(e2_s.at[n, 0], e2_r.at[n, 0], ss.at[9], e_rs.at[n, 2], (s, col(x2, zl)))
        arrived(e1_r.at[n, pl.ds(1, 2)], e_rs.at[n, 1])
        e2_s[n, 1] = (
            e1_r[n, 1].astype(F32) + e1_r[n, 2].astype(F32) + pm[n, col(x, ol)].astype(F32)
        ).astype(BF)
        send(e2_s.at[n, 1], e2_r.at[n, 1], ss.at[9], e_rs.at[n, 2], (s, col(x, ol)))

    def finish(n):
        acc = pm[n, c].astype(F32)
        arrived(e1_r.at[n, pl.ds(0, 4)], e_rs.at[n, 2])
        for i in range(2):
            acc = acc + e1_r[n, 3 + i].astype(F32) + e2_r[n, i].astype(F32)
        fs[n] = acc.astype(BF)
        feature_group(
            far_first[n],
            lambda o, cols: send(
                fs.at[n, :, cols], fo.at[s],
                ss.at[10], d_rs.at[4], (o, c),
            ),
        )

    for n in range(4):
        partial(n)
    deal(dq_s, dq_r, 3)
    combine(0)
    combine(1)
    finish(0)
    combine(2)
    finish(1)
    combine(3)

    dealt(dq_r, 3)
    for t in range(2):
        a = dq_r[2 * t].astype(F32)
        b = dq_r[2 * t + 1].astype(F32)
        tile = slice(t * 128, (t + 1) * 128)
        dq_out[0:128, tile], dq_out[128:256, tile] = halves(a, b)

    finish(2)
    finish(3)
    fo[s] = fs[3, :, my_cols]
    arrived(fo.at[pl.ds(0, 31)], d_rs.at[4])

    dm_out[...] = fo[...]

    for n, ref in enumerate((
        fo.at[pl.ds(0, 31)], kvl.at[pl.ds(0, 3)], kvl.at[pl.ds(0, 3)], kvl.at[pl.ds(0, 3)],
        mem.at[:, pl.ds(0, 7)], kv.at[pl.ds(0, 7)], sb_s, kvl.at[pl.ds(0, 3)],
        e1_r, e2_s, fo.at[pl.ds(0, 31)], rs_s, kvl.at[pl.ds(0, 3)],
    )):
        sent(ref, ss.at[n])


def local(memory, query, out_grad, w_key, w_value):
    dma = pltpu.SemaphoreType.DMA
    v = pltpu.VMEM
    dq, dm = pl.pallas_call(
        kernel,
        out_shape=(
            pltpu.VMEM((256, 256), BF),
            pltpu.VMEM((32, 16, 128), BF),
        ),
        in_specs=[pl.BlockSpec(memory_space=pl.ANY)] * 5,
        out_specs=(pl.BlockSpec(memory_space=pltpu.VMEM),) * 2,
        scratch_shapes=[
            v((4096, 256), BF), v((4096, 256), BF), v((4, 1024, 512), BF),
            v((256, 256), BF), v((256, 256), BF),
            v((4, 8, 16, 1024), BF), v((4, 128, 128), BF),
            v((8, 512, 128), BF), v((8, 128, 512), BF),
            v((4, 128, 128), BF), v((4, 128, 128), BF), v((4, 128, 128), BF), v((4, 128, 128), BF),
            v((128, 1024), BF), v((HD, 1024), F32), v((128, 1024), BF),
            v((512, 1024), F32), v((8, 512, 1024), BF), v((512, 1024), BF),
            v((8, 1024), F32), v((8, 8, 1024), F32), v((8, 1024), F32), v((HD, 1024), F32),
            v((HD, 1024), F32), v((4, 128, 128), F32),
            v((4, 4, 128, 128), BF), v((4, 4, 128, 128), BF),
            v((3, 4, 128, 128), BF), v((3, 4, 128, 128), BF), v((4, 128, 128), F32),
            v((4, 128, 128), BF), v((128, 512), BF),
            v((4, 128, 128), BF), v((4, 128, 128), BF),
            v((4, 8, 16, 1024), BF), v((4, 5, 16, 1024), BF),
            v((4, 2, 16, 1024), BF), v((4, 2, 16, 1024), BF),
            v((4, 16, 1024), BF), v((32, 16, 128), BF),
            dma((5,)), dma((13,)), dma((4,)), dma((4, 3)), dma((17,)), dma((4,)), dma((4,)),
            dma((5,)), dma((4, 3)),
        ],
        compiler_params=pltpu.CompilerParams(
            collective_id=0, has_side_effects=True, vmem_limit_bytes=60 * 1024 * 1024
        ),
    )(memory.reshape(32, 16, 128), query, out_grad, w_key, w_value)
    return dq, dm.reshape(512, 128)


def solution(mesh):
    return jax.shard_map(
        local,
        mesh=mesh,
        in_specs=(
            P("col", "seq"),
            P("seq", "col"),
            P("seq", "col"),
            P(None, "col"),
            P(None, "col"),
        ),
        out_specs=(P("seq", "col"), P("col", "seq")),
        check_vma=False,
    )
```

time: 307 us -> 88.8 us (0.29)
  waiting for transfers between devices: 154 us -> 0 us
  Pallas kernels: 0 us -> 86.8 us
  blocking collectives: 60.9 us -> 0 us
  matrix products: 35 us -> 0 us
  local copies, waits for them, and re-layouts: 22.2 us -> 1.31 us
  between operations: 14.2 us -> 0.64 us
  starting transfers between devices: 9.9 us -> 0 us
  other arithmetic: 9.88 us -> 0 us
    unnamed x3 -> x0, waiting for transfers between devices: 95.6 us -> none
    pallas_call x0 -> x1, Pallas kernels: none -> 86.8 us  [local(): pl.pallas_call(kernel, out_shape=(pltpu.VMEM((256, 256), BF), pltpu.VMEM(...]
    all_to_all x3 -> x0, blocking collectives: 60.9 us -> none  [the longest x1 23.9 us: local(): lax.all_to_all(memory, 'seq', split_axis=0, concat_axis=1, tiled=True)]
    all_gather x1 -> x0, waiting for transfers between devices: 53.9 us -> none  [in_one_piece(): lax.all_gather(both, axis, axis=dim, tiled=True)]
    dot_general x9 -> x0, matrix products: 24.9 us -> none  [the longest x1 7.55 us: local(): jnp.einsum('qhd,khd->hqk', grad_heads, value_heads, preferred_element_typ...]
    split x3 -> x0, local copies, waits for them, and re-layouts: 12.7 us -> none  [in_one_piece(): jnp.split(lax.all_gather(both, axis, axis=dim, tiled=True), ends, axis=al...]
    sub x1 -> x0, matrix products: 10.1 us -> none  [local(): expo = jnp.exp(scores - row_max)]
    all_to_all x1 -> x0, starting transfers between devices: 9.82 us -> none  [local(): lax.all_to_all(summed, 'seq', split_axis=1, concat_axis=0, tiled=True)]
  transfers between devices with their start and end apart: 3 -> 0, of which waited for: 3 -> 0; matrix products, arithmetic and copies ran while one was open for 2% -> 0% of each run, Pallas kernels for 0% -> 0%
where the time goes in v2:
time: 88.8 us; the launch traced here: 88.7 us
  Pallas kernels  86.8 us (98%)
  local copies, waits for them, and re-layouts  1.31 us (1%)
    pallas_call x1, Pallas kernels, local(): pl.pallas_call(kernel, out_shape=(pltpu.VMEM((256, 256), BF), pltpu.VMEM(...  86.8 us

profile of v2, /device:TPU:1, one launch (start us, length us, event | category | flops | bytes accessed | tf_op | source)
XLA Modules:
  0.0 88.7 jit_solution(15124512940600832571)
XLA Ops:
  0.6 86.8 %shard_map.68 = (bf16[256,256]{1,0:T(8,128)(2,1)S(1)}, bf16[32,16,128]{2,1,0:T(8,128)(2,1)S(1)}) custom-call(bf16[32,16,128]{2,1,0:T(8,128)(2,1)} %bitcast.3, bf16[256,256]{1,0:T(8,128)(2,1)} %q_hbm.1, bf16[256,256]{1,0:T(8,128)(2,1)} %g_hbm.1, bf16[4096,256]{1,0:T(8,128)(2,1)} %wk_hbm.1, bf16[4096,256]{1,0:T(8,128)(2,1)} %wv_hbm.1), custom_call_target="tpu_custom_call" | custom-call | tf_op jit(solution)/shard_map/pallas_call | solution.py:468
  87.4 0.7 copy.9
  88.1 0.7 copy.10

commit v3 on v2

--- a/solution.py
+++ b/solution.py
@@ -28,9 +28,9 @@
 
 
 def kernel(
-    mem_hbm, q_hbm, g_hbm, wk_hbm, wv_hbm, dq_out, dm_out,
+    mem_hbm, q_hbm, g_hbm, wk_hbm, wv_hbm, dq_out, dm_out, held,
     wk, wv, wp, qin, gin, mem, kvl, kv, kvt, q_s, q_r, g_s, g_r, qt, gt, gs,
-    sc, ex, ds, mx, tops, ls, att, dqt, gk, sb_s, sb_r, rs_s, rs_r, tot, zb_s, zb, dq_s, dq_r,
+    sc, ex, ds, mx, tops, shr, ls, att, dqt, gk, sb_s, sb_r, rs_s, rs_r, tot, zb_s, hb, pa, dq_s, dq_r,
     pm, e1_r, e2_s, e2_r, fs, fo,
     in_sem, ss, a_rs, b_rs, k_rs, sb_rs, r_rs, d_rs, e_rs,
 ):
@@ -73,37 +73,43 @@
         pl.semaphore_signal(barrier, inc=1, device_id=(s, (c + k) % 8), device_id_type=MESH)
 
     loads = [
-        pltpu.make_async_copy(q_hbm, qin, in_sem.at[0]),
-        pltpu.make_async_copy(g_hbm, gin, in_sem.at[1]),
-        pltpu.make_async_copy(wk_hbm, wk, in_sem.at[2]),
-        pltpu.make_async_copy(wv_hbm, wv, in_sem.at[3]),
+        pltpu.make_async_copy(mem_hbm, held, in_sem.at[5]),
         pltpu.make_async_copy(
             mem_hbm.at[s],
             mem.at[zh, c, :, pl.ds(pl.multiple_of((y * 2 + j) * 128, 128), 128)],
             in_sem.at[4],
         ),
+        pltpu.make_async_copy(q_hbm, qin, in_sem.at[0]),
+        pltpu.make_async_copy(g_hbm, gin, in_sem.at[1]),
+        pltpu.make_async_copy(wk_hbm, wk, in_sem.at[2]),
+        pltpu.make_async_copy(wv_hbm, wv, in_sem.at[3]),
     ]
     for ld in loads:
         ld.start()
 
+    loads[0].wait()
     pl.semaphore_wait(barrier, 38)
 
     my_cols = pl.ds(pl.multiple_of((y * 2 + j) * 128, 128), 128)
     near = (0, 1, 3, 2)
 
+    def far_y(m):
+        at = m // 2
+        return jnp.where(at == 0, 2, jnp.where(at == 1, 1, jnp.where(at == 2, 3, 0)))
+
     def feature_group(dz, act):
-        @pl.loop(0 if dz else 1, 8)
+        @pl.loop(0, 8 if dz else 7)
         def _(m):
-            oy, oc = (y + m // 2) % 4, (j + m) % 2
+            oy, oc = (y + far_y(m)) % 4, (j + 1 + m) % 2
             cols = pl.ds(pl.multiple_of((oy * 2 + oc) * 128, 128), 128)
             act((oy * 4 + (zh + dz) % 4) * 2 + oc, cols)
 
     back = (0, 2, 1, 3)
-    for n, dz in enumerate(near):
+    for n in range(4):
         feature_group(
-            dz,
+            near[n],
             lambda o, cols: send(
-                mem_hbm.at[o], mem.at[zh, c, :, my_cols], ss.at[0], a_rs.at[back[n]], (o, c)
+                held.at[o], mem.at[zh, c, :, my_cols], ss.at[0], a_rs.at[back[n]], (o, c)
             ),
         )
 
@@ -123,7 +129,7 @@
             )
 
     def deal(out, into, which):
-        for k in (1, 3, 2):
+        for k in (2, 1, 3):
             h = (zh + k) % 4
             send(out.at[h], into.at[zh], ss.at[which], d_rs.at[which], at_seq(y, h, j))
         into[zh] = out[zh]
@@ -131,13 +137,13 @@
     def dealt(into, which):
         arrived(into.at[pl.ds(0, 3)], d_rs.at[which])
 
-    loads[0].wait()
-    loads[1].wait()
+    loads[2].wait()
     pack_heads(qin, q_s)
+    loads[3].wait()
     pack_heads(gin, g_s)
 
-    loads[2].wait()
-    loads[3].wait()
+    loads[4].wait()
+    loads[5].wait()
     low_w = lax.broadcasted_iota(jnp.int32, (256, 128), 1) < HD
 
     @pl.loop(0, 16)
@@ -152,7 +158,7 @@
                 low_w, roll64(kt), vt
             ).astype(BF)
 
-    loads[4].wait()
+    loads[1].wait()
 
     def col(xx, zz):
         return xx * 2 + zz
@@ -171,10 +177,10 @@
             arrived(mem.at[quarter(n), c], a_rs.at[n])
         else:
             arrived(fo.at[pl.ds(0, 7)], a_rs.at[n])
+        pass_on(c, n, 1, col(x2, zl))
+        pass_on(c, n, 0, col(x, ol))
         pass_on(c, n, 2, col(x1, zl))
         pass_on(c, n, 2, col(x3, zl))
-        pass_on(c, n, 0, col(x, ol))
-        pass_on(c, n, 1, col(x2, zl))
 
     def relay_near(n):
         arrived(mem.at[quarter(n), 0], b_rs.at[n, 0])
@@ -210,11 +216,10 @@
     def slot(jj, yy, zz):
         return kv.at[jj * 4 + yy, pl.ds(pl.multiple_of(zz * 128, 128), 128)]
 
-    for k in (1, 3, 2):
+    for k in (2, 1, 3):
         h = (zh + k) % 4
         send(kvl.at[h], slot(j, y, zh), ss.at[12], k_rs.at[4 - k], at_seq(y, h, j))
     slot(j, y, zh)[...] = kvl[zh]
-    deal(g_s, g_r, 2)
     y1, y2, y3, oj = (y + 1) % 4, (y + 2) % 4, (y + 3) % 4, 1 - j
 
     def share(yy, zz, sem, to):
@@ -224,6 +229,7 @@
         zz = (zh + k) % 4
         if k:
             arrived(slot(j, y, zz), k_rs.at[k])
+        share(y, zz, 12, at_seq(y2, zh, j))
         share(y, zz, 4 + n, at_seq(y1, zh, j))
         share(y, zz, 8 + n, at_seq(y3, zh, j))
         share(y, zz, 13, at_seq(y, zh, oj))
@@ -244,7 +250,10 @@
             for b in range(4):
                 body(slice(b * 256, (b + 1) * 256))
 
-    def attend(ch):
+    def gather_values(ch, cols):
+        att[:, cols] = att[:, cols] * shr[0:1, cols] + mm(kvt[ch, HD:, :], ex[ch, :, cols])
+
+    def attend(ch, before):
         def score(cols):
             top = jnp.full((8, 256), -jnp.inf, F32)
             for r in range(2):
@@ -256,9 +265,12 @@
             tops[ch, :, cols] = jnp.broadcast_to(top, (8, 256))
 
         def weigh(cols):
+            if before is not None:
+                gather_values(before, cols)
             top = tops[ch, 0:1, cols]
             shrink = jnp.exp2((mx[0:1, cols] - top) * EXP2_SCALE)
             mx[:, cols] = tops[ch, :, cols]
+            shr[:, cols] = jnp.broadcast_to(shrink, (8, 256))
             total = ls[:, cols] * shrink
             for r in range(2):
                 rows = slice(r * 256, (r + 1) * 256)
@@ -266,7 +278,6 @@
                 total = total + e.reshape(32, 8, 256).sum(axis=0)
                 ex[ch, rows, cols] = e.astype(BF)
             ls[:, cols] = total
-            att[:, cols] = att[:, cols] * shrink + mm(kvt[ch, HD:, :], ex[ch, :, cols])
 
         for r in range(2):
             rows = slice(r * 256, (r + 1) * 256)
@@ -274,35 +285,45 @@
         stage(score)
         stage(weigh)
 
-    attend(j * 4 + y)
-    for n, k in enumerate(near):
-        zz = (zh + k) % 4
+    attend(j * 4 + y, None)
+    def forward(n):
+        zz = (zh + near[n]) % 4
         arrived(slot(j, y3, zz), k_rs.at[4 + n])
-        if n < 2:
-            share(y3, zz, 12, at_seq(y1, zh, j))
         share(y3, zz, 16, at_seq(y, zh, oj))
         arrived(slot(j, y1, zz), k_rs.at[8 + n])
-        if n >= 2:
-            share(y1, zz, 12, at_seq(y3, zh, j))
         share(y1, zz, 14, at_seq(y, zh, oj))
 
-    @pl.loop(0, 7)
+    forward(0)
+    forward(1)
+    arrived(kv.at[oj * 4 + y], k_rs.at[13])
+    attend(oj * 4 + y, j * 4 + y)
+    forward(2)
+    forward(3)
+    deal(g_s, g_r, 2)
+
+    def chunk(t):
+        k = jnp.where(t == 2, 3, jnp.where(t == 3, 1, 2))
+        k = jnp.where(t == 5, 3, jnp.where(t == 6, 1, jnp.where(t == 1, 0, k)))
+        own = (t == 2) | (t == 3) | (t == 4)
+        return k, own, jnp.where(own, j, oj) * 4 + (y + k) % 4
+
+    @pl.loop(2, 8)
     def _(i):
-        k = jnp.where(i == 0, 3, jnp.where(i == 1, 1, jnp.where(i == 2, 2, 0)))
-        k = jnp.where(i < 3, k, jnp.where(i == 4, 3, jnp.where(i == 5, 1, jnp.where(i == 6, 2, k))))
-        yy = (y + k) % 4
-
-        @pl.when(i == 1)
+        k, own, now = chunk(i)
+
+        @pl.when(i == 4)
         def _():
             far = kv.at[j * 4 + y2]
             arrived(far, k_rs.at[12])
             send(far, far, ss.at[5], k_rs.at[15], at_seq(y, zh, oj))
 
-        @pl.when(i >= 3)
+        @pl.when(jnp.logical_not(own))
         def _():
-            arrived(kv.at[oj * 4 + yy], k_rs.at[13 + k])
-
-        attend(jnp.where(i < 3, j, oj) * 4 + yy)
+            arrived(kv.at[now], k_rs.at[13 + k])
+
+        attend(now, chunk(i - 1)[2])
+
+    stage(lambda cols: gather_values(oj * 4 + y2, cols))
 
     dealt(g_r, 2)
     gs[0:HD, :] = jnp.zeros((HD, 1024), BF)
@@ -315,8 +336,12 @@
         att[:, cols] = att[:, cols] * inv
     dqt[...] = jnp.zeros((HD, 1024), F32)
 
-    def grads(ch):
+    def query_grad(ch, at, cols):
+        dqt[:, cols] += mm(kvt[ch, 0:HD, :], ds[at, :, cols])
+
+    def grads(ch, before, at):
         def score_grad(cols):
+            query_grad(before, 1 - at, cols)
             shrink = jnp.exp2((tops[ch, 0:1, cols] - mx[0:1, cols]) * EXP2_SCALE)
             scaled = (gt[:, cols] * shrink).astype(BF)
             gs[HD:, cols] = scaled
@@ -324,28 +349,30 @@
             for r in range(2):
                 rows = slice(r * 256, (r + 1) * 256)
                 pg = mm(kv[ch, rows, :], gs[:, cols])
-                ds[rows, cols] = (ex[ch, rows, cols].astype(F32) * (pg - delta)).astype(BF)
-
-        def query_grad(cols):
-            dqt[:, cols] += mm(kvt[ch, 0:HD, :], ds[:, cols])
+                ds[at, rows, cols] = (ex[ch, rows, cols].astype(F32) * (pg - delta)).astype(BF)
 
         stage(score_grad)
-        stage(query_grad)
-        dk = mm_t(qt[0:HD, :], ds[...]) * FACTOR
+        dk = mm_t(qt[0:HD, :], ds[at]) * FACTOR
         dv = mm_t(gs[HD:, :], ex[ch])
         for zz in range(4):
             gk[zz, 0:HD, :] = dk[:, zz * 128 : (zz + 1) * 128]
             gk[zz, HD:, :] = dv[:, zz * 128 : (zz + 1) * 128]
 
-    at_kz = tuple((zh + k) % 4 for k in (1, 3, 2, 0))
-
-    @pl.loop(0, 8)
-    def _(i):
+    ds[1] = jnp.zeros((512, 1024), BF)
+
+    at_kz = tuple((zh + k) % 4 for k in (2, 1, 3, 0))
+
+    def turn(i):
         mine = (i == 2) | (i == 4) | (i == 5) | (i == 7)
         far = jnp.where(i < 4, jnp.where(i == 3, 3, jnp.where(i == 1, 1, 0)), 2)
         k = jnp.where(i == 4, 1, jnp.where(i == 5, 3, far))
+        return mine, k, jnp.where(mine, j, oj) * 4 + (y + 2 + k) % 4
+
+    @pl.loop(0, 8)
+    def _(i):
+        mine, k, now = turn(i)
         yy = (y + 2 + k) % 4
-        grads(jnp.where(mine, j, oj) * 4 + yy)
+        grads(now, turn(jnp.maximum(i - 1, 0))[2], i % 2)
 
         @pl.when(jnp.logical_not(mine))
         def _():
@@ -371,11 +398,6 @@
                         at_seq(yy, zh, j),
                     )
 
-    for b in range(4):
-        pair = [dqt[:, b * 256 + r * 128 : b * 256 + (r + 1) * 128] * FACTOR for r in range(2)]
-        dq_s[b] = jnp.concatenate(pair, axis=0).T.astype(BF)
-
-    head_cols = pl.ds(pl.multiple_of(zh * 128, 128), 128)
     for n, zz in enumerate(at_kz):
         acc = tot[zz]
         arrived(rs_r.at[pl.ds(0, 3), 0], r_rs.at[n])
@@ -383,26 +405,46 @@
             acc = acc + rs_r[k, zz].astype(F32)
         acc = acc.T
         if n < 3:
+            k = (2, 1, 3)[n]
             zb_s[zz] = acc.astype(BF)
-            send(zb_s.at[zz], zb.at[:, head_cols], ss.at[7], d_rs.at[0], at_seq(y, zz, j))
+            send(zb_s.at[zz], hb.at[4 - k], ss.at[7], d_rs.at[8 - k], at_seq(y, zz, j))
         else:
-            zb[:, head_cols] = acc.astype(BF)
-
-    arrived(zb.at[:, pl.ds(0, 384)], d_rs.at[0])
-    lhs = zb[...]
+            hb[0] = acc.astype(BF)
+
+    stage(lambda cols: query_grad(j * 4 + y, 1, cols))
+    for b in range(4):
+        pair = [dqt[:, b * 256 + r * 128 : b * 256 + (r + 1) * 128] * FACTOR for r in range(2)]
+        dq_s[b] = jnp.concatenate(pair, axis=0).T.astype(BF)
+
     far_first = (2, 3, 1, 0)
 
+    def head_part(n, r, o):
+        cols = pl.ds(pl.multiple_of((zh + o) % 4 * 128, 128), 128)
+        return mm_t(hb[o], wp[(zh + far_first[n]) % 4, r * 512 : (r + 1) * 512, cols])
+
+    for n in range(4):
+        for r in range(2):
+            pa[n, :, r * 512 : (r + 1) * 512] = head_part(n, r, 0)
+
+    @pl.loop(0, 2)
+    def _(i):
+        o = 1 + 2 * i
+        arrived(hb.at[o], d_rs.at[4 + o])
+        for n in range(4):
+            for r in range(2):
+                pa[n, :, r * 512 : (r + 1) * 512] += head_part(n, r, o)
+
+    arrived(hb.at[2], d_rs.at[6])
+
     def partial(n):
-        zq = (zh + far_first[n]) % 4
         for r in range(2):
-            part = mm_t(lhs, wp[zq, r * 512 : (r + 1) * 512, :]).astype(BF)
-            pm[n, :, :, r * 512 : (r + 1) * 512] = part.reshape(8, 16, 512)
+            cols = slice(r * 512, (r + 1) * 512)
+            part = pa[n, :, cols] + head_part(n, r, 2)
+            pm[n, :, :, cols] = part.astype(BF).reshape(8, 16, 512)
         for i, (block, to) in enumerate((
             (col(x2, ol), col(x, ol)),
             (col(x1, ol), col(x1, zl)),
             (col(x3, ol), col(x3, zl)),
-            (col(x1, zl), col(x1, zl)),
-            (col(x3, zl), col(x3, zl)),
         )):
             send(pm.at[n, block], e1_r.at[n, i], ss.at[8], e_rs.at[n, (i + 1) // 2], (s, to))
 
@@ -415,6 +457,8 @@
             e1_r[n, 1].astype(F32) + e1_r[n, 2].astype(F32) + pm[n, col(x, ol)].astype(F32)
         ).astype(BF)
         send(e2_s.at[n, 1], e2_r.at[n, 1], ss.at[9], e_rs.at[n, 2], (s, col(x, ol)))
+        for i, to in ((3, col(x1, zl)), (4, col(x3, zl))):
+            send(pm.at[n, to], e1_r.at[n, i], ss.at[8], e_rs.at[n, 2], (s, to))
 
     def finish(n):
         acc = pm[n, c].astype(F32)
@@ -440,6 +484,8 @@
     finish(1)
     combine(3)
 
+    finish(2)
+    finish(3)
     dealt(dq_r, 3)
     for t in range(2):
         a = dq_r[2 * t].astype(F32)
@@ -447,8 +493,6 @@
         tile = slice(t * 128, (t + 1) * 128)
         dq_out[0:128, tile], dq_out[128:256, tile] = halves(a, b)
 
-    finish(2)
-    finish(3)
     fo[s] = fs[3, :, my_cols]
     arrived(fo.at[pl.ds(0, 31)], d_rs.at[4])
 
@@ -474,30 +518,54 @@
         in_specs=[pl.BlockSpec(memory_space=pl.ANY)] * 5,
         out_specs=(pl.BlockSpec(memory_space=pltpu.VMEM),) * 2,
         scratch_shapes=[
+            v((32, 16, 128), BF),
             v((4096, 256), BF), v((4096, 256), BF), v((4, 1024, 512), BF),
             v((256, 256), BF), v((256, 256), BF),
             v((4, 8, 16, 1024), BF), v((4, 128, 128), BF),
             v((8, 512, 128), BF), v((8, 128, 512), BF),
             v((4, 128, 128), BF), v((4, 128, 128), BF), v((4, 128, 128), BF), v((4, 128, 128), BF),
             v((128, 1024), BF), v((HD, 1024), F32), v((128, 1024), BF),
-            v((512, 1024), F32), v((8, 512, 1024), BF), v((512, 1024), BF),
-            v((8, 1024), F32), v((8, 8, 1024), F32), v((8, 1024), F32), v((HD, 1024), F32),
+            v((512, 1024), F32), v((8, 512, 1024), BF), v((2, 512, 1024), BF),
+            v((8, 1024), F32), v((8, 8, 1024), F32), v((8, 1024), F32), v((8, 1024), F32), v((HD, 1024), F32),
             v((HD, 1024), F32), v((4, 128, 128), F32),
             v((4, 4, 128, 128), BF), v((4, 4, 128, 128), BF),
             v((3, 4, 128, 128), BF), v((3, 4, 128, 128), BF), v((4, 128, 128), F32),
-            v((4, 128, 128), BF), v((128, 512), BF),
+            v((4, 128, 128), BF), v((4, 128, 128), BF), v((4, 128, 1024), F32),
             v((4, 128, 128), BF), v((4, 128, 128), BF),
             v((4, 8, 16, 1024), BF), v((4, 5, 16, 1024), BF),
             v((4, 2, 16, 1024), BF), v((4, 2, 16, 1024), BF),
             v((4, 16, 1024), BF), v((32, 16, 128), BF),
-            dma((5,)), dma((13,)), dma((4,)), dma((4, 3)), dma((17,)), dma((4,)), dma((4,)),
-            dma((5,)), dma((4, 3)),
+            dma((6,)), dma((13,)), dma((4,)), dma((4, 3)), dma((17,)), dma((4,)), dma((4,)),
+            dma((8,)), dma((4, 3)),
         ],
         compiler_params=pltpu.CompilerParams(
             collective_id=0, has_side_effects=True, vmem_limit_bytes=60 * 1024 * 1024
         ),
     )(memory.reshape(32, 16, 128), query, out_grad, w_key, w_value)
-    return dq, dm.reshape(512, 128)
+    return pl.pallas_call(
+        write_out,
+        out_shape=(
+            jax.ShapeDtypeStruct((256, 256), BF),
+            jax.ShapeDtypeStruct((512, 128), BF),
+        ),
+        in_specs=[pl.BlockSpec(memory_space=pltpu.VMEM)] * 2,
+        out_specs=(pl.BlockSpec(memory_space=pl.ANY),) * 2,
+        scratch_shapes=[pltpu.SemaphoreType.DMA((2,))],
+    )(
+        pltpu.with_memory_space_constraint(dq, pltpu.VMEM),
+        pltpu.with_memory_space_constraint(dm.reshape(512, 128), pltpu.VMEM),
+    )
+
+
+def write_out(dq_ref, dm_ref, dq_out, dm_out, sem):
+    copies = [
+        pltpu.make_async_copy(dq_ref, dq_out, sem.at[0]),
+        pltpu.make_async_copy(dm_ref, dm_out, sem.at[1]),
+    ]
+    for copy in copies:
+        copy.start()
+    for copy in copies:
+        copy.wait()
 
 
 def solution(mesh):

time: 88.8 us -> 82.5 us (0.929)
  Pallas kernels: 86.8 us -> 81.8 us
  local copies, waits for them, and re-layouts: 1.31 us -> 0 us
    pallas_call x1, Pallas kernels: 86.8 us -> 81.1 us  [local(): pl.pallas_call(kernel, out_shape=(pltpu.VMEM((256, 256), BF), pltpu.VMEM(...]
    unnamed x2 -> x0, local copies, waits for them, and re-layouts: 1.31 us -> none
where the time goes in v3:
time: 82.5 us
  Pallas kernels  81.8 us (99%)
    pallas_call x1, Pallas kernels, local(): pl.pallas_call(kernel, out_shape=(pltpu.VMEM((256, 256), BF), pltpu.VMEM(...  81.1 us

profile of v3, /device:TPU:1, one launch (start us, length us, event | category | flops | bytes accessed | tf_op | source)
XLA Modules:
  0.0 82.5 jit_solution(17183433554377861319)
XLA Ops:
  0.6 81.1 %shard_map.68 = (bf16[256,256]{1,0:T(8,128)(2,1)S(1)}, bf16[32,16,128]{2,1,0:T(8,128)(2,1)S(1)}) custom-call(bf16[32,16,128]{2,1,0:T(8,128)(2,1)} %bitcast.3, bf16[256,256]{1,0:T(8,128)(2,1)} %q_hbm.1, bf16[256,256]{1,0:T(8,128)(2,1)} %g_hbm.1, bf16[4096,256]{1,0:T(8,128)(2,1)} %wk_hbm.1, bf16[4096,256]{1,0:T(8,128)(2,1)} %wv_hbm.1), custom_call_target="tpu_custom_call" | custom-call | tf_op jit(solution)/shard_map/pallas_call | solution.py:512
  81.7 0.7 shard_map.69

commit v4 on v3

--- a/solution.py
+++ b/solution.py
@@ -196,13 +196,13 @@
     relay_near(0)
     own_rows(2)
     relay_near(1)
+    relay_far(0)
     own_rows(3)
     deal(q_s, q_r, 1)
-    relay_far(0)
     relay_near(2)
     relay_far(1)
+    relay_far(2)
     relay_near(3)
-    relay_far(2)
     relay_far(3)
 
     kv_new = jnp.zeros((128, 512), F32)
@@ -476,14 +476,11 @@
 
     for n in range(4):
         partial(n)
+    for n in range(4):
+        combine(n)
     deal(dq_s, dq_r, 3)
-    combine(0)
-    combine(1)
     finish(0)
-    combine(2)
     finish(1)
-    combine(3)
-
     finish(2)
     finish(3)
     dealt(dq_r, 3)

time: 82.5 us -> 79.5 us (0.964)
  Pallas kernels: 81.8 us -> 78.8 us
    pallas_call x1, Pallas kernels: 81.1 us -> 78.1 us  [local(): pl.pallas_call(kernel, out_shape=(pltpu.VMEM((256, 256), BF), pltpu.VMEM(...]
where the time goes in v4:
time: 79.5 us; the launch traced here: 79.4 us
  Pallas kernels  78.8 us (99%)
    pallas_call x1, Pallas kernels, local(): pl.pallas_call(kernel, out_shape=(pltpu.VMEM((256, 256), BF), pltpu.VMEM(...  78.1 us

profile of v4, /device:TPU:1, one launch (start us, length us, event | category | flops | bytes accessed | tf_op | source)
XLA Modules:
  0.0 79.4 jit_solution(7524064022833306921)
XLA Ops:
  0.6 78.1 %shard_map.68 = (bf16[256,256]{1,0:T(8,128)(2,1)S(1)}, bf16[32,16,128]{2,1,0:T(8,128)(2,1)S(1)}) custom-call(bf16[32,16,128]{2,1,0:T(8,128)(2,1)} %bitcast.3, bf16[256,256]{1,0:T(8,128)(2,1)} %q_hbm.1, bf16[256,256]{1,0:T(8,128)(2,1)} %g_hbm.1, bf16[4096,256]{1,0:T(8,128)(2,1)} %wk_hbm.1, bf16[4096,256]{1,0:T(8,128)(2,1)} %wv_hbm.1), custom_call_target="tpu_custom_call" | custom-call | tf_op jit(solution)/shard_map/pallas_call | solution.py:509
  78.7 0.7 shard_map.69

commit v5 on v4

--- a/solution.py
+++ b/solution.py
@@ -198,9 +198,9 @@
     relay_near(1)
     relay_far(0)
     own_rows(3)
-    deal(q_s, q_r, 1)
     relay_near(2)
     relay_far(1)
+    deal(q_s, q_r, 1)
     relay_far(2)
     relay_near(3)
     relay_far(3)

time: 79.5 us -> 79.9 us (level)
  no operation moved by 1% of the time
where the time goes in v5:
time: 79.9 us; the launch traced here: 79.8 us
  Pallas kernels  79.2 us (99%)
    pallas_call x1, Pallas kernels, local(): pl.pallas_call(kernel, out_shape=(pltpu.VMEM((256, 256), BF), pltpu.VMEM(...  78.5 us

profile of v5, /device:TPU:1, one launch (start us, length us, event | category | flops | bytes accessed | tf_op | source)
XLA Modules:
  0.0 79.8 jit_solution(6677085731309657505)
XLA Ops:
  0.6 78.5 %shard_map.68 = (bf16[256,256]{1,0:T(8,128)(2,1)S(1)}, bf16[32,16,128]{2,1,0:T(8,128)(2,1)S(1)}) custom-call(bf16[32,16,128]{2,1,0:T(8,128)(2,1)} %bitcast.3, bf16[256,256]{1,0:T(8,128)(2,1)} %q_hbm.1, bf16[256,256]{1,0:T(8,128)(2,1)} %g_hbm.1, bf16[4096,256]{1,0:T(8,128)(2,1)} %wk_hbm.1, bf16[4096,256]{1,0:T(8,128)(2,1)} %wv_hbm.1), custom_call_target="tpu_custom_call" | custom-call | tf_op jit(solution)/shard_map/pallas_call | solution.py:509
  79.1 0.7 shard_map.69
